TPU v7x, 32 devices: a whole 2x2x4 slice. The times are simulated.
32 devices in a mesh: occ: 8 (over y, x, core), ao: 4 (over z).
Axes of the slice: x: 2, y: 2, z: 4, core: 2. Of those that a mesh axis runs over, the one named last changes fastest.
Arguments:
- coef: bfloat16 [2048, 8], P('ao', 'occ'), may hold values from -0.5 to 0.5
- half_ints: bfloat16 [8, 1024, 2048], P('occ', None, 'ao'), may hold values from -0.5 to 0.5
- metric_inv: bfloat16 [64, 128, 128], replicated, may hold values from -1 to 2, as said below
- dom_blocks: int32 [8, 8], P('occ'), may hold values from 0 to 63, as said below
- dom_len: int32 [8], P('occ'), may hold values from 2 to 8
Outputs:
- exchange_k: float32 [2048, 2048], P('ao', 'occ')
- fit_density: float32 [8192], replicated
Inputs may be any that keep to these rules, and one draw needn't show every extreme that they name: `dom_blocks`: each row holds 8 different block numbers. `metric_inv`: full rank blocks.
All inputs are finite; a program needn't handle non-finite values.
Results may differ from a plain program's by a relative error of at most 0.0055.
Values may be sent and summed in bfloat16 or wider, within the bound.
No kernel may reach another device: no remote copies, remote signals or barrier semaphores. Data moves between devices by JAX's collectives and lax.ppermute only.
A program may use at most 128 MiB of HBM per device.

v0:
```python
import jax
import jax.numpy as jnp
from jax import lax
from jax.sharding import PartitionSpec as P


def on_device(coef, half_ints, metric_inv, dom_blocks, dom_len):
    lmo_count, domain, ao_rows = half_ints.shape
    block = metric_inv.shape[1]
    slots = domain // block
    fit_blocks = metric_inv.shape[0]
    metric_rows = metric_inv[dom_blocks]
    raw_ints = half_ints.reshape(lmo_count, slots, block, ao_rows)
    fitted = jnp.einsum(
        "isab,isbm->isam", metric_rows, raw_ints, preferred_element_type=jnp.float32
    )
    live_slots = jnp.arange(slots, dtype=jnp.int32)[None, :] < dom_len[:, None]
    fitted = jnp.where(live_slots[:, :, None, None], fitted, 0.0)
    fitted = fitted.reshape(lmo_count, domain, ao_rows).astype(jnp.bfloat16)
    pair_part = jnp.einsum("ipm,mi->ip", fitted, coef, preferred_element_type=jnp.float32)
    one_hot = (
        dom_blocks[:, :, None] == jnp.arange(fit_blocks, dtype=jnp.int32)[None, None, :]
    ).astype(jnp.float32)
    local_density = jnp.einsum("isf,isr->fr", one_hot, pair_part.reshape(lmo_count, slots, block))
    density = lax.psum(local_density, ("occ", "ao"))
    density = density.reshape(fit_blocks * block)
    partial_value = jnp.einsum(
        "ipm,ipn->mn",
        fitted,
        lax.all_gather(fitted, "ao", axis=2, tiled=True),
        preferred_element_type=jnp.float32,
    )
    exchange_k = lax.psum_scatter(partial_value, "occ", scatter_dimension=1, tiled=True)
    return (exchange_k, density)


def solution(mesh):
    in_specs = (P("ao", "occ"), P("occ", None, "ao"), P(), P("occ", None), P("occ"))
    out_specs = (P("ao", "occ"), P())
    return jax.shard_map(
        on_device, mesh=mesh, in_specs=in_specs, out_specs=out_specs, check_vma=False
    )
```

profile of v0, /device:TPU:0, one launch (start us, length us, event | category | flops | bytes accessed | tf_op | source)
XLA Modules:
  0.0 159.3 jit_solution(12443113816982479165)
XLA Ops:
  7.2 0.0 copy-start
  7.2 0.0 all-gather.2.cloned.1.call-start
  8.0 0.7 fusion.5
  8.7 0.1 copy-done
  8.8 0.6 gather_fusion
  9.4 2.7 %select_convert_fusion = bf16[8,128,512]{2,1,0:T(8,128)(2,1)} fusion(bf16[8,128,128]{2,1,0:T(8,128)(2,1)S(1)} %gather_fusion, bf16[8,128,512]{2,1,0:T(8,128)(2,1)} %bitcast.25, pred[8]{0:T(512)(128)(4,1)S(1)} %iota_compare_fusion.2), kind=kOutput, calls=%fused_computation.3 | convolution fusion | flops 135266304 | bytes 2359304 | tf_op jit(solution)/shard_map/isab,isbm->isam/dot_general | solution.py:14
  12.1 0.0 all-gather.2.cloned.1.call-update
  12.1 0.0 reduce-scatter.2.cloned.1.call-start
  12.1 83.6 %all-gather.2.cloned.1.call-done = bf16[1,1024,2048]{2,1,0:T(8,128)(2,1)} async-done(((bf16[1,1024,512]{2,1,0:T(8,128)(2,1)}), bf16[1,1024,2048]{2,1,0:T(8,128)(2,1)}) %all-gather.2.cloned.1.call-update) | async-done | bytes 4194320 | tf_op jit(solution)/shard_map/all_gather | solution.py:30
  95.7 6.8 %fusion = f32[512,2048]{1,0:T(8,128)} fusion(bf16[1024,512]{1,0:T(8,128)(2,1)} %bitcast.24, bf16[1,1024,2048]{2,1,0:T(8,128)(2,1)} %all-gather.2.cloned.1.call-done), kind=kOutput, calls=%fused_computation.1 | convolution fusion | flops 2147483648 | bytes 9437184 | tf_op jit(solution)/shard_map/ipm,ipn->mn/dot_general | solution.py:27
  102.5 0.0 copy-start.1
  102.5 0.0 copy-start.2
  102.5 0.0 copy-start.3
  102.5 0.0 reduce-scatter.2.cloned.1.call-update
  102.6 1.2 copy-done.1
  103.8 0.0 copy-done.2
  103.8 0.4 fusion.2
  104.1 0.0 copy-done.3
  104.1 0.3 convolution_bitcast_fusion
  104.4 39.3 %psum.7 = f32[8192]{0:T(1024)} all-reduce(f32[8192]{0:T(1024)S(1)} %convolution_bitcast_fusion), channel_id=1, replica_groups=mesh['occ'=8,'ao'=4] {'occ','ao'}, use_global_device_ids=true, to_apply=%region_1.2 | all-reduce | flops 8192 | bytes 65536 | tf_op jit(solution)/shard_map/psum | solution.py:25
  143.7 8.8 %reduce-scatter.2.cloned.1.call-done = f32[512,256]{1,0:T(8,128)} async-done(((f32[512,2048]{1,0:T(8,128)}), f32[512,256]{1,0:T(8,128)}) %reduce-scatter.2.cloned.1.call-update) | async-done | bytes 524304 | tf_op jit(solution)/shard_map/reduce_scatter | solution.py:33
  (2 shorter events, 0.0 us)
Async XLA Ops:
  7.2 1.6 %copy-start = (bf16[64,128,128]{2,1,0:T(8,128)(2,1)S(1)}, bf16[64,128,128]{2,1,0:T(8,128)(2,1)}, u32[]{:S(2)}) copy-start(bf16[64,128,128]{2,1,0:T(8,128)(2,1)} %param.7) | copy-start | bytes 6291460
  7.2 88.5 %all-gather.2.cloned.1.call-start = ((), (), s32[]{:S(2)}) async-start(), calls=%async_computation.1 | async-start | bytes 5242880 | tf_op jit(solution)/shard_map/all_gather | solution.py:30
  12.1 140.4 %reduce-scatter.2.cloned.1.call-start = ((), (), s32[]{:S(2)}) async-start(), calls=%async_computation.2 | async-start | bytes 4718592 | tf_op jit(solution)/shard_map/reduce_scatter | solution.py:33
  102.5 1.2 copy-start.1
  102.5 1.2 copy-start.2
  102.5 1.6 copy-start.3
Sparse Core Ops, SparseCore 0:
  12.2 83.4 all-gather.1
  102.7 49.7 reduce-scatter.1
where the time goes:
time: 160 us; the launch traced here: 159 us
  waiting for transfers between devices  92.3 us (58%)
  blocking collectives  39.3 us (25%)
  between operations  14.8 us (9%)
  matrix products  10.2 us (6%)
  local copies, waits for them, and re-layouts  1.89 us (1%)
    all_gather x1, waiting for transfers between devices, on_device(): lax.all_gather(fitted, 'ao', axis=2, tiled=True)  83.6 us
    psum x1, blocking collectives, on_device(): density = lax.psum(local_density, ('occ', 'ao'))  39.3 us
    reduce_scatter x1, waiting for transfers between devices, on_device(): lax.psum_scatter(partial_value, 'occ', scatter_dimension=1, tiled=True)  8.75 us
    dot_general x1, matrix products, on_device(): jnp.einsum('ipm,ipn->mn', fitted, lax.all_gather(fitted, 'ao', axis=2, ti...  6.82 us
  transfers between devices with their start and end apart: 2, of which 2 were waited for; matrix products, arithmetic and copies ran while one was open for 0% of the time, Pallas kernels for 0%

commit v1 on v0

--- a/solution.py
+++ b/solution.py
@@ -22,7 +22,8 @@
         dom_blocks[:, :, None] == jnp.arange(fit_blocks, dtype=jnp.int32)[None, None, :]
     ).astype(jnp.float32)
     local_density = jnp.einsum("isf,isr->fr", one_hot, pair_part.reshape(lmo_count, slots, block))
-    density = lax.psum(local_density, ("occ", "ao"))
+    blocks = lax.all_gather(local_density, ("occ", "ao"))
+    density = jnp.sum(blocks, axis=0)
     density = density.reshape(fit_blocks * block)
     partial_value = jnp.einsum(
         "ipm,ipn->mn",

time: 160 us -> 212 us (1.32)
  waiting for transfers between devices: 92.3 us -> 182 us
  blocking collectives: 39.3 us -> 0 us
    all_gather x0 -> x1, waiting for transfers between devices: none -> 49 us  [on_device(): blocks = lax.all_gather(local_density, ('occ', 'ao'))]
    reduce_scatter x1, waiting for transfers between devices: 8.75 us -> 52.1 us  [on_device(): lax.psum_scatter(partial_value, 'occ', scatter_dimension=1, tiled=True)]
    psum x1 -> x0, blocking collectives: 39.3 us -> none  [on_device(): density = lax.psum(local_density, ('occ', 'ao'))]
    all_gather x1, waiting for transfers between devices: 83.6 us -> 81 us  [on_device(): lax.all_gather(fitted, 'ao', axis=2, tiled=True)]
  transfers between devices with their start and end apart: 2 -> 3, of which waited for: 2 -> 3; matrix products, arithmetic and copies ran while one was open for 0% -> 5% of each run, Pallas kernels for 0% -> 0%
where the time goes in v1:
time: 212 us
  waiting for transfers between devices  182 us (86%)
  between operations  14.6 us (7%)
  matrix products  12 us (6%)
  other arithmetic  2.58 us (1%)
    all_gather x1, waiting for transfers between devices, on_device(): lax.all_gather(fitted, 'ao', axis=2, tiled=True)  81 us
    reduce_scatter x1, waiting for transfers between devices, on_device(): lax.psum_scatter(partial_value, 'occ', scatter_dimension=1, tiled=True)  52.1 us
    all_gather x1, waiting for transfers between devices, on_device(): blocks = lax.all_gather(local_density, ('occ', 'ao'))  49 us
    dot_general x1, matrix products, on_device(): jnp.einsum('ipm,ipn->mn', fitted, lax.all_gather(fitted, 'ao', axis=2, ti...  6.86 us
  transfers between devices with their start and end apart: 3, of which 3 were waited for; matrix products, arithmetic and copies ran while one was open for 5% of the time, Pallas kernels for 0%

profile of v1, /device:TPU:0, one launch (start us, length us, event | category | flops | bytes accessed | tf_op | source)
XLA Modules:
  0.0 212.0 jit_solution(1869800519201846238)
XLA Ops:
  7.2 0.0 copy-start
  7.2 0.0 copy-start.1
  7.2 0.0 all-gather.4.cloned.1.call-start
  8.0 0.7 fusion.6
  8.7 0.1 copy-done
  8.8 0.6 gather_fusion
  9.4 2.6 %select_convert_fusion = bf16[8,128,512]{2,1,0:T(8,128)(2,1)} fusion(bf16[8,128,128]{2,1,0:T(8,128)(2,1)S(1)} %gather_fusion, bf16[8,128,512]{2,1,0:T(8,128)(2,1)} %bitcast.25, pred[8]{0:T(512)(128)(4,1)S(1)} %iota_compare_fusion.2), kind=kOutput, calls=%fused_computation.3 | convolution fusion | flops 135266304 | bytes 2359304 | tf_op jit(solution)/shard_map/isab,isbm->isam/dot_general | solution.py:14
  12.0 0.0 all-gather.4.cloned.1.call-update
  12.0 0.0 all-gather.6.cloned.1.call-start
  12.1 1.6 fusion.3
  13.7 0.0 copy-done.1
  13.7 0.9 fusion.2
  14.6 0.0 all-gather.6.cloned.1.call-update
  14.6 0.0 reduce-scatter.2.cloned.1.call-start
  14.6 81.0 %all-gather.4.cloned.1.call-done = bf16[1,1024,2048]{2,1,0:T(8,128)(2,1)} async-done(((bf16[1,1024,512]{2,1,0:T(8,128)(2,1)}), bf16[1,1024,2048]{2,1,0:T(8,128)(2,1)}) %all-gather.4.cloned.1.call-update) | async-done | bytes 4194320 | tf_op jit(solution)/shard_map/all_gather | solution.py:31
  95.6 6.9 %fusion = f32[512,2048]{1,0:T(8,128)} fusion(bf16[1024,512]{1,0:T(8,128)(2,1)} %bitcast.24, bf16[1,1024,2048]{2,1,0:T(8,128)(2,1)} %all-gather.4.cloned.1.call-done), kind=kOutput, calls=%fused_computation.1 | convolution fusion | flops 2147483648 | bytes 9437184 | tf_op jit(solution)/shard_map/ipm,ipn->mn/dot_general | solution.py:28
  102.5 0.0 reduce-scatter.2.cloned.1.call-update
  102.5 49.0 %all-gather.6.cloned.1.call-done = f32[2048,128]{1,0:T(8,128)} async-done(((f32[64,128]{1,0:T(8,128)}), f32[2048,128]{1,0:T(8,128)}) %all-gather.6.cloned.1.call-update) | async-done | bytes 1048592 | tf_op jit(solution)/shard_map/all_gather | solution.py:25
  151.5 1.9 reduce_sum.9
  153.4 52.1 %reduce-scatter.2.cloned.1.call-done = f32[512,256]{1,0:T(8,128)} async-done(((f32[512,2048]{1,0:T(8,128)}), f32[512,256]{1,0:T(8,128)}) %reduce-scatter.2.cloned.1.call-update) | async-done | bytes 524304 | tf_op jit(solution)/shard_map/reduce_scatter | solution.py:34
  (2 shorter events, 0.0 us)
Async XLA Ops:
  7.2 1.6 copy-start
  7.2 6.5 %copy-start.1 = (s32[1,8]{1,0:T(1,128)S(1)}, s32[1,8]{1,0:T(1,128)}, u32[]{:S(2)}) copy-start(s32[1,8]{1,0:T(1,128)} %param.8) | copy-start | bytes 100
  7.2 88.4 %all-gather.4.cloned.1.call-start = ((), (), s32[]{:S(2)}) async-start(), calls=%async_computation.1 | async-start | bytes 5242880 | tf_op jit(solution)/shard_map/all_gather | solution.py:31
  12.0 139.5 %all-gather.6.cloned.1.call-start = ((), (), s32[]{:S(2)}) async-start(), calls=%async_computation.3 | async-start | bytes 1081344 | tf_op jit(solution)/shard_map/all_gather | solution.py:25
  14.6 190.9 %reduce-scatter.2.cloned.1.call-start = ((), (), s32[]{:S(2)}) async-start(), calls=%async_computation.2 | async-start | bytes 4718592 | tf_op jit(solution)/shard_map/reduce_scatter | solution.py:34
Sparse Core Ops, SparseCore 0:
  12.1 83.4 all-gather.3
  99.2 52.2 all-gather.5
  155.4 50.0 reduce-scatter.1

commit v2 on v0

--- a/solution.py
+++ b/solution.py
@@ -22,7 +22,9 @@
         dom_blocks[:, :, None] == jnp.arange(fit_blocks, dtype=jnp.int32)[None, None, :]
     ).astype(jnp.float32)
     local_density = jnp.einsum("isf,isr->fr", one_hot, pair_part.reshape(lmo_count, slots, block))
-    density = lax.psum(local_density, ("occ", "ao"))
+    density = local_density
+    for mesh_axis in ("ao", "occ"):
+        density = lax.psum(density, mesh_axis)
     density = density.reshape(fit_blocks * block)
     partial_value = jnp.einsum(
         "ipm,ipn->mn",

time: 160 us -> 160 us (level)
    psum x1 -> x2, blocking collectives: 39.3 us -> 40.2 us  [on_device(): density = lax.psum(density, mesh_axis)]
where the time goes in v2:
time: 160 us; the launch traced here: 159 us
  waiting for transfers between devices  91.7 us (57%)
  blocking collectives  40.2 us (25%)
  between operations  14.9 us (9%)
  matrix products  10.2 us (6%)
  local copies, waits for them, and re-layouts  1.89 us (1%)
    all_gather x1, waiting for transfers between devices, on_device(): lax.all_gather(fitted, 'ao', axis=2, tiled=True)  83.6 us
    psum x2, blocking collectives, on_device(): density = lax.psum(density, mesh_axis)  40.2 us
    reduce_scatter x1, waiting for transfers between devices, on_device(): lax.psum_scatter(partial_value, 'occ', scatter_dimension=1, tiled=True)  8.08 us
    dot_general x1, matrix products, on_device(): jnp.einsum('ipm,ipn->mn', fitted, lax.all_gather(fitted, 'ao', axis=2, ti...  6.82 us
  transfers between devices with their start and end apart: 2, of which 2 were waited for; matrix products, arithmetic and copies ran while one was open for 0% of the time, Pallas kernels for 0%

profile of v2, /device:TPU:0, one launch (start us, length us, event | category | flops | bytes accessed | tf_op | source)
XLA Modules:
  0.0 159.5 jit_solution(2553503244912495583)
XLA Ops:
  7.2 0.0 copy-start
  7.2 0.0 all-gather.2.cloned.1.call-start
  8.0 0.7 fusion.6
  8.7 0.1 copy-done
  8.8 0.6 gather_fusion
  9.4 2.7 %select_convert_fusion = bf16[8,128,512]{2,1,0:T(8,128)(2,1)} fusion(bf16[8,128,128]{2,1,0:T(8,128)(2,1)S(1)} %gather_fusion, bf16[8,128,512]{2,1,0:T(8,128)(2,1)} %bitcast.24, pred[8]{0:T(512)(128)(4,1)S(1)} %iota_compare_fusion.2), kind=kOutput, calls=%fused_computation.3 | convolution fusion | flops 135266304 | bytes 2359304 | tf_op jit(solution)/shard_map/isab,isbm->isam/dot_general | solution.py:14
  12.1 0.0 all-gather.2.cloned.1.call-update
  12.1 0.0 reduce-scatter.2.cloned.1.call-start
  12.2 83.6 %all-gather.2.cloned.1.call-done = bf16[1,1024,2048]{2,1,0:T(8,128)(2,1)} async-done(((bf16[1,1024,512]{2,1,0:T(8,128)(2,1)}), bf16[1,1024,2048]{2,1,0:T(8,128)(2,1)}) %all-gather.2.cloned.1.call-update) | async-done | bytes 4194320 | tf_op jit(solution)/shard_map/all_gather | solution.py:32
  95.7 6.8 %fusion = f32[512,2048]{1,0:T(8,128)} fusion(bf16[1024,512]{1,0:T(8,128)(2,1)} %bitcast.23, bf16[1,1024,2048]{2,1,0:T(8,128)(2,1)} %all-gather.2.cloned.1.call-done), kind=kOutput, calls=%fused_computation.1 | convolution fusion | flops 2147483648 | bytes 9437184 | tf_op jit(solution)/shard_map/ipm,ipn->mn/dot_general | solution.py:29
  102.5 0.0 copy-start.1
  102.5 0.0 copy-start.2
  102.5 0.0 copy-start.3
  102.5 0.0 reduce-scatter.2.cloned.1.call-update
  102.6 1.2 copy-done.1
  103.8 0.0 copy-done.2
  103.8 0.4 fusion.3
  104.1 0.0 copy-done.3
  104.1 0.3 fusion.2
  104.4 16.3 %psum.14 = f32[64,128]{1,0:T(8,128)S(1)} all-reduce(f32[64,128]{1,0:T(8,128)S(1)} %fusion.2), channel_id=1, replica_groups=mesh['occ'=8,'ao'=4] {'ao'}, use_global_device_ids=true, to_apply=%region_1.2 | all-reduce | flops 8192 | bytes 65536 | tf_op jit(solution)/shard_map/psum | solution.py:27
  120.7 23.8 %psum.15 = f32[8192]{0:T(1024)} all-reduce(f32[8192]{0:T(1024)S(1)} %bitcast.25), channel_id=1, replica_groups=mesh['occ'=8,'ao'=4] {'occ'}, use_global_device_ids=true, to_apply=%region_2.3 | all-reduce | flops 8192 | bytes 65536 | tf_op jit(solution)/shard_map/psum | solution.py:27
  144.6 8.1 %reduce-scatter.2.cloned.1.call-done = f32[512,256]{1,0:T(8,128)} async-done(((f32[512,2048]{1,0:T(8,128)}), f32[512,256]{1,0:T(8,128)}) %reduce-scatter.2.cloned.1.call-update) | async-done | bytes 524304 | tf_op jit(solution)/shard_map/reduce_scatter | solution.py:35
  (2 shorter events, 0.0 us)
Async XLA Ops:
  7.2 1.6 %copy-start = (bf16[64,128,128]{2,1,0:T(8,128)(2,1)S(1)}, bf16[64,128,128]{2,1,0:T(8,128)(2,1)}, u32[]{:S(2)}) copy-start(bf16[64,128,128]{2,1,0:T(8,128)(2,1)} %param.7) | copy-start | bytes 6291460
  7.2 88.5 %all-gather.2.cloned.1.call-start = ((), (), s32[]{:S(2)}) async-start(), calls=%async_computation.1 | async-start | bytes 5242880 | tf_op jit(solution)/shard_map/all_gather | solution.py:32
  12.1 140.6 %reduce-scatter.2.cloned.1.call-start = ((), (), s32[]{:S(2)}) async-start(), calls=%async_computation.2 | async-start | bytes 4718592 | tf_op jit(solution)/shard_map/reduce_scatter | solution.py:35
  102.5 1.2 copy-start.1
  102.5 1.2 copy-start.2
  102.5 1.6 copy-start.3
Sparse Core Ops, SparseCore 0:
  12.2 83.4 all-gather.1
  102.7 49.9 reduce-scatter.1
